TPU v7x, 512 devices: a whole 4x8x8 slice. The times are simulated.
512 devices in a mesh: row: 16 (over y, core), col: 32 (over z, x).
Axes of the slice: x: 4, y: 8, z: 8, core: 2. Of those that a mesh axis runs over, the one named last changes fastest.
Arguments:
- points: bfloat16 [128, 65536], P(None, ('row', 'col')), may hold values from -6 to 6
- inv_scale: float32 [128], replicated, may hold values from 0.07 to 0.22
- basis: bfloat16 [65536, 4096], P(('row', 'col')), may hold values from -0.25 to 0.25
- shrink: float32 [4096], replicated, may hold values from 0.02 to 1
- solution: float32 [33, 65536], P(None, ('row', 'col')), may hold values from -6 to 6
- residual: float32 [33, 65536], P(None, ('row', 'col')), may hold values from -6 to 6
- direction_prev: float32 [33, 65536], P(None, ('row', 'col')), may hold values from -6 to 6
- rz_prev: float32 [33], replicated, may hold values from 65536 to 262144
Outputs:
- solution_next: float32 [33, 65536], P(None, ('row', 'col'))
- residual_next: float32 [33, 65536], P(None, ('row', 'col'))
- direction: float32 [33, 65536], P(None, ('row', 'col'))
All inputs are finite; a program needn't handle non-finite values.
Results may differ from a plain program's by a relative error of at most 0.019.
Values may be sent and summed in bfloat16 or wider, within the bound.
A program may use at most 64 MiB of HBM per device.

v0:
```python
import jax
import jax.numpy as jnp
from jax import lax
from jax.sharding import PartitionSpec as P

noise_level = 0.25


def local(points, inv_scale, basis, shrink, solution, residual, direction_prev, rz_prev):
    scaled = (points * inv_scale[:, None]).astype(jnp.bfloat16)
    residual_bf = residual.astype(jnp.bfloat16)
    local_proj = jnp.dot(residual_bf, basis, preferred_element_type=jnp.float32)
    damping = shrink - 1.0
    projected = lax.psum(local_proj, ("row", "col"))
    correction = (damping[None, :] * projected).astype(jnp.bfloat16)
    precond = residual + jnp.dot(correction, basis.T, preferred_element_type=jnp.float32)
    precond_inner = lax.psum(jnp.sum(residual * precond, axis=1), ("row", "col"))
    direction = precond + (precond_inner / rz_prev)[:, None] * direction_prev
    direction_bf = direction.astype(jnp.bfloat16)
    row_points = lax.all_gather(scaled, "col", axis=1, tiled=True)
    row_sq = jnp.sum(jnp.square(row_points.astype(jnp.float32)), axis=0)
    rows_total = row_points.shape[1]
    width = min(1024, rows_total)
    direction_piece = lax.all_gather(direction_bf, "row", axis=1, tiled=True)
    column_pts = lax.all_gather(scaled, "row", axis=1, tiled=True)
    column_sq = jnp.sum(jnp.square(column_pts.astype(jnp.float32)), axis=0)
    results = []
    for offset in range(0, rows_total, width):
        rows = row_points[:, offset : offset + width]
        cross = lax.dot_general(
            column_pts, rows, (((0,), (0,)), ((), ())), preferred_element_type=jnp.float32
        )
        distance = jnp.maximum(
            column_sq[:, None] + row_sq[None, offset : offset + width] - 2.0 * cross, 0.0
        )
        tile = jnp.exp(-0.5 * distance).astype(jnp.bfloat16)
        results.append(jnp.dot(direction_piece, tile, preferred_element_type=jnp.float32))
    image_part = jnp.concatenate(results, axis=1)
    image = (
        lax.psum_scatter(
            image_part.astype(jnp.bfloat16), "col", scatter_dimension=1, tiled=True
        ).astype(jnp.float32)
        + noise_level * direction
    )
    curvature = lax.psum(jnp.sum(direction * image, axis=1), ("row", "col"))
    alpha = precond_inner / curvature
    solution_next = solution + alpha[:, None] * direction
    residual_next = residual - alpha[:, None] * image
    return (solution_next, residual_next, direction)


def solution(mesh):
    placed = (
        P(None, ("row", "col")),
        P(),
        P(("row", "col"), None),
        P(),
        P(None, ("row", "col")),
        P(None, ("row", "col")),
        P(None, ("row", "col")),
        P(),
    )
    return jax.shard_map(
        local,
        mesh=mesh,
        in_specs=placed,
        out_specs=(P(None, ("row", "col")), P(None, ("row", "col")), P(None, ("row", "col"))),
        check_vma=False,
    )
```

profile of v0, /device:TPU:1, one launch (start us, length us, event | category | flops | bytes accessed | tf_op | source)
XLA Modules:
  0.0 740.1 jit_solution(11344339179035116326)
XLA Ops:
  8.0 0.0 copy-start
  8.0 0.0 copy-start.4
  8.0 0.0 copy-start.8
  8.0 0.0 all-reduce.2.cloned.1.call-start
  8.1 1.2 copy-done
  9.2 1.9 fusion.17
  11.1 0.0 copy-start.7
  11.1 0.0 copy-start.3
  11.1 0.0 all-reduce.2.cloned.1.call-update
  11.1 0.0 all-gather.2.cloned.1.call-start
  11.2 0.0 copy-done.4
  11.2 0.0 copy-done.8
  11.2 0.7 multiply_convert_fusion.2
  11.9 0.0 all-gather.2.cloned.1.call-update
  11.9 0.0 reduce-scatter.4.cloned.1.call-start
  11.9 22.7 %all_gather.10 = bf16[128,2048]{1,0:T(8,128)(2,1)S(1)} all-gather(bf16[128,128]{1,0:T(8,128)(2,1)} %multiply_convert_fusion.2), channel_id=1, replica_groups=mesh['row'=16,'col'=32] {'row'}, dimensions={1}, use_global_device_ids=true | all-gather | bytes 557056 | tf_op jit(solution)/shard_map/all_gather | solution.py:25
  34.6 0.0 copy-start.9
  34.6 0.0 copy-start.6
  34.6 0.1 multiply_reduce_fusion.1
  34.8 0.0 copy-done.7
  34.8 256.8 %all-reduce.2.cloned.1.call-done = f32[33,4096]{1,0:T(8,128)} async-done(((f32[33,4096]{1,0:T(8,128)}), f32[33,4096]{1,0:T(8,128)}) %all-reduce.2.cloned.1.call-update) | async-done | bytes 540688 | tf_op jit(solution)/shard_map/psum | solution.py:14
  291.6 0.0 copy-done.3
  291.6 1.7 multiply_reduce_fusion.3
  293.3 97.0 %psum.22 = f32[33]{0:T(128)S(1)} all-reduce(f32[33]{0:T(128)S(1)} %get-tuple-element.11), channel_id=1, replica_groups=mesh['row'=16,'col'=32] {'row','col'}, use_global_device_ids=true, to_apply=%region_2.0 | all-reduce | flops 33 | bytes 264 | tf_op jit(solution)/shard_map/psum | solution.py:17
  390.3 0.0 copy-done.9
  390.3 0.0 copy-done.6
  390.3 0.1 fusion.31
  390.4 0.0 copy-start.2
  390.4 15.4 %all_gather.9 = bf16[33,2048]{1,0:T(8,128)(2,1)S(1)} all-gather(bf16[33,128]{1,0:T(8,128)(2,1)S(1)} %get-tuple-element.3), channel_id=1, replica_groups=mesh['row'=16,'col'=32] {'row'}, dimensions={1}, use_global_device_ids=true | all-gather | bytes 143616 | tf_op jit(solution)/shard_map/all_gather | solution.py:24
  405.7 0.0 all-gather.2.cloned.1.call-done
  405.7 0.0 copy-start.1
  405.7 1.5 multiply_reduce_fusion
  407.3 0.0 copy-done.1
  407.3 2.7 fusion.4
  410.0 2.7 fusion.5
  412.7 2.7 fusion.6
  415.5 2.7 fusion.7
  418.2 0.0 copy-start.5
  418.2 1.4 copy.11
  419.6 0.0 reduce-scatter.4.cloned.1.call-update
  419.7 210.6 %reduce-scatter.4.cloned.1.call-done = bf16[128,33]{1,0:T(8,128)(2,1)} async-done(((bf16[4096,33]{1,0:T(8,128)(2,1)}), bf16[128,33]{1,0:T(8,128)(2,1)}) %reduce-scatter.4.cloned.1.call-update) | async-done | bytes 8464
  630.3 0.8 copy.12
  631.1 0.1 multiply_reduce_fusion.2
  631.2 100.7 %psum.23 = f32[33]{0:T(128)S(1)} all-reduce(f32[33]{0:T(128)S(1)} %multiply_reduce_fusion.2), channel_id=1, replica_groups=mesh['row'=16,'col'=32] {'row','col'}, use_global_device_ids=true, to_apply=%region_7.0 | all-reduce | flops 33 | bytes 264 | tf_op jit(solution)/shard_map/psum | solution.py:45
  731.9 0.0 copy-done.2
  731.9 0.0 copy-done.5
  731.9 0.7 multiply_subtract_fusion
  (5 shorter events, 0.0 us)
Async XLA Ops:
  8.0 1.2 copy-start
  8.0 3.2 copy-start.4
  8.0 3.2 copy-start.8
  8.0 283.6 %all-reduce.2.cloned.1.call-start = ((), (), s32[]{:S(2)}) async-start(), calls=%async_computation.1 | async-start | bytes 1310720 | tf_op jit(solution)/shard_map/psum | solution.py:14
  11.1 23.7 %copy-start.7 = (f32[4096]{0:T(1024)S(1)}, f32[4096]{0:T(1024)}, u32[]{:S(2)}) copy-start(f32[4096]{0:T(1024)} %param.11) | copy-start | bytes 49156
  11.1 280.5 %copy-start.3 = (f32[33,128]{1,0:T(8,128)S(1)}, f32[33,128]{1,0:T(8,128)}, u32[]{:S(2)}) copy-start(f32[33,128]{1,0:T(8,128)} %param.13) | copy-start | bytes 50692
  11.1 394.6 %all-gather.2.cloned.1.call-start = ((), (), s32[]{:S(2)}) async-start(), calls=%async_computation.2 | async-start | bytes 1081344 | tf_op jit(solution)/shard_map/all_gather | solution.py:20
  11.9 618.4 %reduce-scatter.4.cloned.1.call-start = ((), (), s32[]{:S(2)}) async-start(), calls=%async_computation.3 | async-start | bytes 1081344
  34.6 355.6 %copy-start.9 = (f32[33]{0:T(128)S(1)}, f32[33]{0:T(128)}, u32[]{:S(2)}) copy-start(f32[33]{0:T(128)} %param.15) | copy-start | bytes 400
  34.6 355.6 %copy-start.6 = (f32[33,128]{1,0:T(8,128)S(1)}, f32[33,128]{1,0:T(8,128)}, u32[]{:S(2)}) copy-start(f32[33,128]{1,0:T(8,128)} %param.14) | copy-start | bytes 50692
  390.4 341.6 %copy-start.2 = (f32[33,128]{1,0:T(8,128)}, f32[33,128]{1,0:T(8,128)S(1)}, u32[]{:S(2)}) copy-start(f32[33,128]{1,0:T(8,128)S(1)} %get-tuple-element.4) | copy-start | bytes 50692
  405.7 1.6 copy-start.1
  418.2 313.7 %copy-start.5 = (f32[33,128]{1,0:T(8,128)S(1)}, f32[33,128]{1,0:T(8,128)}, u32[]{:S(2)}) copy-start(f32[33,128]{1,0:T(8,128)} %param.12) | copy-start | bytes 50692
Sparse Core Ops, SparseCore 0:
  13.8 277.7 all-reduce.1
Sparse Core Ops, SparseCore 1:
  15.1 78.6 all-gather.1
  419.7 210.5 reduce-scatter.3
where the time goes:
time: 740 us
  waiting for transfers between devices  467 us (63%)
  blocking collectives  236 us (32%)
  between operations  15.6 us (2%)
  matrix products  14.4 us (2%)
    psum x1, waiting for transfers between devices, local(): projected = lax.psum(local_proj, ('row', 'col'))  257 us
    unnamed x4, waiting for transfers between devices  211 us
    psum x1, blocking collectives, local(): curvature = lax.psum(jnp.sum(direction * image, axis=1), ('row', 'col'))  101 us
    psum x1, blocking collectives, local(): lax.psum(jnp.sum(residual * precond, axis=1), ('row', 'col'))  97 us
    all_gather x1, blocking collectives, local(): column_pts = lax.all_gather(scaled, 'row', axis=1, tiled=True)  22.7 us
    all_gather x1, blocking collectives, local(): direction_piece = lax.all_gather(direction_bf, 'row', axis=1, tiled=True)  15.4 us
  transfers between devices with their start and end apart: 3, of which 2 were waited for; matrix products, arithmetic and copies ran while one was open for 0% of the time, Pallas kernels for 0%

commit v1 on v0

--- a/solution.py
+++ b/solution.py
@@ -22,7 +22,16 @@
     rows_total = row_points.shape[1]
     width = min(1024, rows_total)
     direction_piece = lax.all_gather(direction_bf, "row", axis=1, tiled=True)
-    column_pts = lax.all_gather(scaled, "row", axis=1, tiled=True)
+    ways = lax.axis_size("row")
+    up = [(d, (d + 1) % ways) for d in range(ways)]
+    down = [(d, (d - 1) % ways) for d in range(ways)]
+    earlier, later = ([scaled], [scaled])
+    for _ in range(ways // 2):
+        earlier.append(lax.ppermute(earlier[-1], "row", up))
+    for _ in range((ways - 1) // 2):
+        later.append(lax.ppermute(later[-1], "row", down))
+    line = jnp.concatenate([*earlier[::-1], *later[1:]], axis=1)
+    column_pts = jnp.roll(line, (lax.axis_index("row") - ways // 2) * scaled.shape[1], axis=1)
     column_sq = jnp.sum(jnp.square(column_pts.astype(jnp.float32)), axis=0)
     results = []
     for offset in range(0, rows_total, width):

time: 740 us -> 744 us (level)
  starting transfers between devices: 0.13 us -> 29.6 us
  blocking collectives: 236 us -> 213 us
    ppermute x0 -> x15, starting transfers between devices: none -> 29.5 us  [the longest x7 26.8 us: local(): later.append(lax.ppermute(later[-1], 'row', down))]
    all_gather x1 -> x0, blocking collectives: 22.7 us -> none  [local(): column_pts = lax.all_gather(scaled, 'row', axis=1, tiled=True)]
    psum x1, waiting for transfers between devices: 257 us -> 240 us  [local(): projected = lax.psum(local_proj, ('row', 'col'))]
    ppermute x0 -> x15, waiting for transfers between devices: none -> 10.4 us  [the longest x8 8.66 us: local(): earlier.append(lax.ppermute(earlier[-1], 'row', up))]
  transfers between devices with their start and end apart: 3 -> 18, of which waited for: 2 -> 16; matrix products, arithmetic and copies ran while one was open for 0% -> 0% of each run, Pallas kernels for 0% -> 0%
where the time goes in v1:
time: 744 us
  waiting for transfers between devices  462 us (62%)
  blocking collectives  213 us (29%)
  starting transfers between devices  29.6 us (4%)
  between operations  15.8 us (2%)
  matrix products  15.6 us (2%)
    psum x1, waiting for transfers between devices, local(): projected = lax.psum(local_proj, ('row', 'col'))  240 us
    unnamed x4, waiting for transfers between devices  211 us
    psum x1, blocking collectives, local(): curvature = lax.psum(jnp.sum(direction * image, axis=1), ('row', 'col'))  101 us
    psum x1, blocking collectives, local(): lax.psum(jnp.sum(residual * precond, axis=1), ('row', 'col'))  97 us
    ppermute x7, starting transfers between devices, local(): later.append(lax.ppermute(later[-1], 'row', down))  26.8 us
    all_gather x1, blocking collectives, local(): direction_piece = lax.all_gather(direction_bf, 'row', axis=1, tiled=True)  15.5 us
  transfers between devices with their start and end apart: 18, of which 16 were waited for; matrix products, arithmetic and copies ran while one was open for 0% of the time, Pallas kernels for 0%

profile of v1, /device:TPU:1, one launch (start us, length us, event | category | flops | bytes accessed | tf_op | source)
XLA Modules:
  0.0 743.9 jit_solution(16294866178107994062)
XLA Ops:
  8.0 0.0 copy-start
  8.0 0.0 all-reduce.2.cloned.1.call-start
  8.1 1.1 copy-done
  9.2 1.8 fusion.25
  11.1 0.0 all-reduce.2.cloned.1.call-update
  11.1 0.0 all-gather.2.cloned.1.call-start
  11.2 0.1 multiply_convert_fusion.2
  11.3 2.7 collective-permute-start
  14.0 4.9 collective-permute-done
  18.9 0.0 collective-permute-start.1
  18.9 3.8 collective-permute-start.8
  22.7 0.7 collective-permute-done.1
  23.4 0.0 collective-permute-start.2
  23.4 0.2 collective-permute-done.8
  23.6 3.7 collective-permute-start.9
  27.3 0.7 collective-permute-done.2
  28.0 0.0 collective-permute-start.3
  28.0 0.2 collective-permute-done.9
  28.1 3.7 collective-permute-start.10
  31.8 0.7 collective-permute-done.3
  32.5 0.0 collective-permute-start.4
  32.5 0.2 collective-permute-done.10
  32.7 3.7 collective-permute-start.11
  36.4 0.7 collective-permute-done.4
  37.1 0.0 collective-permute-start.5
  37.1 0.2 collective-permute-done.11
  37.2 3.7 collective-permute-start.12
  41.0 0.7 collective-permute-done.5
  41.6 0.0 collective-permute-start.6
  41.6 0.0 all-gather.2.cloned.1.call-update
  41.7 0.0 reduce-scatter.4.cloned.1.call-start
  41.7 0.1 collective-permute-done.12
  41.8 4.0 collective-permute-start.13
  45.9 0.3 collective-permute-done.6
  46.2 0.0 collective-permute-start.7
  46.2 0.5 collective-permute-done.13
  46.7 4.1 collective-permute-start.14
  50.8 0.0 collective-permute-done.7
  51.0 0.0 copy-start.4
  51.0 0.1 constant_dynamic-update-slice_fusion.23
  51.2 0.5 collective-permute-done.14
  51.8 0.1 constant_dynamic-update-slice_fusion.7
  52.1 0.0 copy-start.10
  52.1 0.0 copy-start.7
  52.1 0.1 multiply_reduce_fusion.1
  52.2 240.4 %all-reduce.2.cloned.1.call-done = f32[33,4096]{1,0:T(8,128)} async-done(((f32[33,4096]{1,0:T(8,128)}), f32[33,4096]{1,0:T(8,128)}) %all-reduce.2.cloned.1.call-update) | async-done | bytes 540688 | tf_op jit(solution)/shard_map/psum | solution.py:14
  292.6 1.7 multiply_reduce_fusion.3
  294.3 97.0 %psum.22 = f32[33]{0:T(128)S(1)} all-reduce(f32[33]{0:T(128)S(1)} %get-tuple-element.11), channel_id=1, replica_groups=mesh['row'=16,'col'=32] {'row','col'}, use_global_device_ids=true, to_apply=%region_2.0 | all-reduce | flops 33 | bytes 264 | tf_op jit(solution)/shard_map/psum | solution.py:17
  391.3 0.1 fusion.47
  391.4 15.5 %all_gather.6 = bf16[33,2048]{1,0:T(8,128)(2,1)S(1)} all-gather(bf16[33,128]{1,0:T(8,128)(2,1)S(1)} %get-tuple-element.3), channel_id=1, replica_groups=mesh['row'=16,'col'=32] {'row'}, dimensions={1}, use_global_device_ids=true | all-gather | bytes 143616 | tf_op jit(solution)/shard_map/all_gather | solution.py:24
  406.9 1.5 multiply_reduce_fusion
  408.5 2.7 fusion.7
  411.2 2.7 fusion.6
  413.9 3.4 fusion.5
  417.3 3.3 fusion.4
  420.6 0.9 pad_maximum_fusion
  421.6 0.0 copy-start.6
  421.6 1.4 copy.11
  423.0 0.0 reduce-scatter.4.cloned.1.call-update
  423.0 211.0 %reduce-scatter.4.cloned.1.call-done = bf16[128,33]{1,0:T(8,128)(2,1)} async-done(((bf16[4096,33]{1,0:T(8,128)(2,1)}), bf16[128,33]{1,0:T(8,128)(2,1)}) %reduce-scatter.4.cloned.1.call-update) | async-done | bytes 8464
  634.1 0.8 copy.12
  634.9 0.1 multiply_reduce_fusion.2
  635.0 100.7 %psum.23 = f32[33]{0:T(128)S(1)} all-reduce(f32[33]{0:T(128)S(1)} %multiply_reduce_fusion.2), channel_id=1, replica_groups=mesh['row'=16,'col'=32] {'row','col'}, use_global_device_ids=true, to_apply=%region_7.8 | all-reduce | flops 33 | bytes 264 | tf_op jit(solution)/shard_map/psum | solution.py:54
  735.7 0.7 multiply_subtract_fusion
  (51 shorter events, 0.4 us)
Async XLA Ops:
  8.0 1.2 copy-start
  8.0 3.1 copy-start.2
  8.0 3.1 copy-start.9
  8.0 38.2 %copy-start.8 = (f32[4096]{0:T(1024)S(1)}, f32[4096]{0:T(1024)}, u32[]{:S(2)}) copy-start(f32[4096]{0:T(1024)} %param.11) | copy-start | bytes 49156
  8.0 284.6 %all-reduce.2.cloned.1.call-start = ((), (), s32[]{:S(2)}) async-start(), calls=%async_computation.1 | async-start | bytes 1310720 | tf_op jit(solution)/shard_map/psum | solution.py:14
  11.1 395.8 %all-gather.2.cloned.1.call-start = ((), (), s32[]{:S(2)}) async-start(), calls=%async_computation.2 | async-start | bytes 1081344 | tf_op jit(solution)/shard_map/all_gather | solution.py:20
  11.3 30.4 %copy-start.5 = (bf16[128,128]{1,0:T(8,128)(2,1)}, bf16[128,128]{1,0:T(8,128)(2,1)S(1)}, u32[]{:S(2)}) copy-start(bf16[128,128]{1,0:T(8,128)(2,1)S(1)} %multiply_convert_fusion.2) | copy-start | bytes 98308
  11.3 7.6 %collective-permute-start = (bf16[128,128]{1,0:T(8,128)(2,1)S(1)}, bf16[128,128]{1,0:T(8,128)(2,1)S(1)}, u32[]{:S(2)}, u32[]{:S(2)}) collective-permute-start(bf16[128,128]{1,0:T(8,128)(2,1)S(1)} %multiply_convert_fusion.2), channel_id=1, source_target_pairs={{0,32},{32,64},{64,96},{96,128},{128,160},{160,192},{192,224},{224... | collective-permute-start | bytes 98312 | tf_op jit(solution)/shard_map/ppermute | solution.py:30
  18.9 4.5 collective-permute-start.1
  18.9 4.7 collective-permute-start.8
  23.4 4.6 collective-permute-start.2
  23.6 4.6 collective-permute-start.9
  28.0 4.6 collective-permute-start.3
  28.1 4.6 collective-permute-start.10
  32.5 4.6 collective-permute-start.4
  32.7 4.6 collective-permute-start.11
  37.1 4.6 collective-permute-start.5
  37.2 4.6 collective-permute-start.12
  41.6 4.6 collective-permute-start.6
  41.7 592.4 %reduce-scatter.4.cloned.1.call-start = ((), (), s32[]{:S(2)}) async-start(), calls=%async_computation.3 | async-start | bytes 1081344
  41.8 4.9 collective-permute-start.13
  46.2 4.6 collective-permute-start.7
  46.7 4.9 collective-permute-start.14
  51.0 241.6 %copy-start.4 = (f32[33,128]{1,0:T(8,128)S(1)}, f32[33,128]{1,0:T(8,128)}, u32[]{:S(2)}) copy-start(f32[33,128]{1,0:T(8,128)} %param.13) | copy-start | bytes 50692
  52.1 339.2 %copy-start.10 = (f32[33]{0:T(128)S(1)}, f32[33]{0:T(128)}, u32[]{:S(2)}) copy-start(f32[33]{0:T(128)} %param.15) | copy-start | bytes 400
  52.1 339.2 %copy-start.7 = (f32[33,128]{1,0:T(8,128)S(1)}, f32[33,128]{1,0:T(8,128)}, u32[]{:S(2)}) copy-start(f32[33,128]{1,0:T(8,128)} %param.14) | copy-start | bytes 50692
  391.4 344.4 %copy-start.3 = (f32[33,128]{1,0:T(8,128)}, f32[33,128]{1,0:T(8,128)S(1)}, u32[]{:S(2)}) copy-start(f32[33,128]{1,0:T(8,128)S(1)} %get-tuple-element.4) | copy-start | bytes 50692
  406.9 1.6 copy-start.1
  421.6 314.1 %copy-start.6 = (f32[33,128]{1,0:T(8,128)S(1)}, f32[33,128]{1,0:T(8,128)}, u32[]{:S(2)}) copy-start(f32[33,128]{1,0:T(8,128)} %param.12) | copy-start | bytes 50692
Sparse Core Ops, SparseCore 0:
  13.8 278.7 all-reduce.1
Sparse Core Ops, SparseCore 1:
  41.8 76.3 all-gather.1
  423.1 210.9 reduce-scatter.3
